TPU v7x, 32 devices: a whole 2x2x4 slice. The times are simulated.
32 devices in a mesh: dp: 2 (over y), seq: 16 (over z, x, core).
Axes of the slice: x: 2, y: 2, z: 4, core: 2. Of those that a mesh axis runs over, the one named last changes fastest.
Arguments:
- frame_in: bfloat16 [2, 2304, 1024], P('dp', 'seq'), may hold values from -120 to 120
- token_ids: int32 [2, 16, 60], P('dp', 'seq'), may hold values from 0 to 1663
- durations: int32 [2, 16, 60], P('dp', 'seq'), may hold values from 1 to 4, 144 in all within a row
- valid_len: int32 [2], P('dp'), may hold values from 576 to 2304, as said below
- t_bin: int32 [2], P('dp'), may hold values from 0 to 63
- token_table: bfloat16 [1664, 512], P('seq'), may hold values from -6 to 6
- enc_weight: bfloat16 [512, 1024], replicated, may hold values from -0.25 to 0.25
- mod_table: float32 [64, 2048], replicated, may hold values from -1.2 to 2.5
- w_query: bfloat16 [1024, 512], P('seq'), may hold values from -0.1875 to 0.1875
- w_key: bfloat16 [1024, 512], P('seq'), may hold values from -0.1875 to 0.1875
- w_value: bfloat16 [1024, 512], P('seq'), may hold values from -0.1875 to 0.1875
- attn_grad: bfloat16 [2, 2304, 512], P('dp', 'seq'), may hold values from -6 to 6
Outputs:
- attn_out: bfloat16 [2, 2304, 512], P('dp', 'seq')
- frame_grad: bfloat16 [2, 2304, 1024], P('dp', 'seq')
- query_weight_grad: float32 [1024, 512], P('seq')
- key_weight_grad: float32 [1024, 512], P('seq')
- value_weight_grad: float32 [1024, 512], P('seq')
Inputs may be any that keep to these rules, and one draw needn't show every extreme that they name: In every slab the 60 durations sum to 144, so each token's frames lie in its own slab; some token lasts 4 frames. `valid_len`: some recording is valid over all 2304 frames.
All inputs are finite; a program needn't handle non-finite values.
Results may differ from a plain program's by a relative error of at most 0.017.
The roundings to bfloat16 on the way count: a program that leaves them out, or rounds other values in their place, can miss the bound.
Values may be sent and summed in bfloat16 or wider, within the bound.
No kernel may reach another device: no remote copies, remote signals or barrier semaphores. Data moves between devices by JAX's collectives and lax.ppermute only.
A program may use at most 64 MiB of HBM per device.

v0:
```python
import math
import jax
import jax.numpy as jnp
from jax import lax
from jax.sharding import PartitionSpec as P

D = 1024
HEADS = 8
HD = 64
BLK = 48
QW = 512


def shifted(block, axis, distance):
    devices = range(lax.axis_size(axis))
    route = [(i - distance, i) for i in devices if i - distance in devices]
    return lax.ppermute(block, axis, route)


def attend_window(
    q_blocks, key_ext, value_ext, grad_out, query_pos, key_pos, valid_end, frames_total
):
    n_blocks = q_blocks.shape[0]
    block_len = q_blocks.shape[1]
    key_win = jnp.concatenate([key_ext[offset : offset + n_blocks] for offset in range(4)], axis=1)
    value_win = jnp.concatenate(
        [value_ext[offset : offset + n_blocks] for offset in range(4)], axis=1
    )
    key_here = key_pos[:, None, :]
    allowed = (
        (key_here >= 0)
        & (key_here < frames_total)
        & ((key_here < valid_end) | (query_pos[:, :, None] >= valid_end))
    )
    row_mask = allowed[:, None]
    inv_scale = 1.0 / math.sqrt(q_blocks.shape[-1])
    scores = (
        jnp.einsum("bqhd,bkhd->bhqk", q_blocks, key_win, preferred_element_type=jnp.float32)
        * inv_scale
    )
    scores = jnp.where(row_mask, scores, -1e30)
    row_top = jnp.max(scores, axis=-1, keepdims=True)
    shifted_exp = jnp.where(row_mask, jnp.exp(scores - row_top), 0.0)
    attn_prob = shifted_exp / jnp.sum(shifted_exp, axis=-1, keepdims=True)
    probs_low = attn_prob.astype(jnp.bfloat16)
    mixed_out = jnp.einsum(
        "bhqk,bkhd->bqhd", probs_low, value_win, preferred_element_type=jnp.float32
    ).astype(jnp.bfloat16)
    grad_probs = jnp.einsum(
        "bqhd,bkhd->bhqk", grad_out, value_win, preferred_element_type=jnp.float32
    )
    centre = jnp.sum(attn_prob * grad_probs, axis=-1, keepdims=True)
    grad_scores = (attn_prob * (grad_probs - centre) * inv_scale).astype(jnp.bfloat16)
    grad_query = jnp.einsum(
        "bhqk,bkhd->bqhd", grad_scores, key_win, preferred_element_type=jnp.float32
    ).astype(jnp.bfloat16)
    key_terms = jnp.einsum(
        "bhqk,bqhd->bkhd", grad_scores, q_blocks, preferred_element_type=jnp.float32
    )
    value_terms = jnp.einsum(
        "bhqk,bqhd->bkhd", probs_low, grad_out, preferred_element_type=jnp.float32
    )
    win_terms = jnp.concatenate([key_terms, value_terms], axis=2)
    pieces = win_terms.reshape(n_blocks, 4, block_len, win_terms.shape[2], win_terms.shape[3])
    folded = jnp.zeros((n_blocks + 3,) + pieces.shape[2:], jnp.float32)
    for offset in range(4):
        folded = folded + jnp.pad(pieces[:, offset], ((offset, 3 - offset), (0, 0), (0, 0), (0, 0)))
    return (mixed_out, grad_query, folded)


def pick_rows(wanted, table_piece):
    inside = (wanted >= 0) & (wanted < table_piece.shape[0])
    picked = jnp.take(table_piece, jnp.clip(wanted, 0, table_piece.shape[0] - 1), axis=0)
    return jnp.where(inside[:, None], picked, jnp.zeros_like(picked))


def shards(
    frame_in,
    token_ids,
    durations,
    valid_len,
    t_bin,
    token_table,
    enc_weight,
    mod_table,
    w_query,
    w_key,
    w_value,
    attn_grad,
):
    frames = frame_in[0]
    n_frames = frames.shape[0]
    seq_count = lax.axis_size("seq")
    seq_index = lax.axis_index("seq")
    dp_count = lax.axis_size("dp")
    frames_total = n_frames * seq_count
    valid_end = valid_len[0]
    wanted = token_ids[0, 0]
    token_emb = pick_rows(wanted, lax.all_gather(token_table, "seq", axis=0, tiled=True))
    token_ends = jnp.cumsum(durations[0, 0])
    local_pos = jnp.arange(n_frames, dtype=jnp.int32)
    owner_tok = jnp.sum((token_ends[None, :] <= local_pos[:, None]).astype(jnp.int32), axis=1)
    frame_emb = jnp.take(token_emb, owner_tok, axis=0)
    hidden_in = frames.astype(jnp.float32) + jnp.dot(
        frame_emb, enc_weight, preferred_element_type=jnp.float32
    )
    root_ms = jnp.sqrt(jnp.mean(hidden_in * hidden_in, axis=1, keepdims=True) + 1e-06)
    normed = hidden_in / root_ms
    modulation = lax.dynamic_index_in_dim(mod_table, t_bin[0], 0, keepdims=False)
    gain_part = 1.0 + modulation[:D]
    shift_part = modulation[D:]
    modulated = (normed * gain_part + shift_part).astype(jnp.bfloat16)
    shard_cat = jnp.concatenate([w_query, w_key, w_value], axis=1)
    weights_all = lax.all_gather(shard_cat, "seq", axis=0, tiled=True)
    projected = jnp.dot(modulated, weights_all, preferred_element_type=jnp.float32).astype(
        jnp.bfloat16
    )
    queries = projected[:, :QW]
    keys_values = projected[:, QW:]
    before_rim = shifted(keys_values[n_frames - 2 * BLK :], "seq", 1)
    after_rim = shifted(keys_values[:BLK], "seq", -1)
    extended = jnp.concatenate([before_rim, keys_values, after_rim], axis=0)
    n_blocks = n_frames // BLK
    ext_blocks = extended.reshape(n_blocks + 3, BLK, 2, HEADS, HD)
    global_pos = seq_index * n_frames + local_pos
    query_pos = global_pos.reshape(n_blocks, BLK)
    key_pos = (
        seq_index * n_frames
        + (jnp.arange(n_blocks, dtype=jnp.int32)[:, None] - 2) * BLK
        + jnp.arange(4 * BLK, dtype=jnp.int32)[None, :]
    )
    live_rows = global_pos < valid_end
    grad_live = jnp.where(live_rows[:, None], attn_grad[0], jnp.zeros_like(attn_grad[0]))
    attn_blocks, query_grad, ext_grad = attend_window(
        queries.reshape(n_blocks, BLK, HEADS, HD),
        ext_blocks[:, :, 0],
        ext_blocks[:, :, 1],
        grad_live.reshape(n_blocks, BLK, HEADS, HD),
        query_pos,
        key_pos,
        valid_end,
        frames_total,
    )
    ext_rows = ext_grad.reshape(n_frames + 3 * BLK, 2 * QW)
    from_next = shifted(ext_rows[: 2 * BLK], "seq", -1)
    from_prev = shifted(ext_rows[n_frames + 2 * BLK :], "seq", 1)
    own_rows = ext_rows[2 * BLK : 2 * BLK + n_frames]
    own_rows = (
        own_rows
        + jnp.pad(from_next, ((n_frames - 2 * BLK, 0), (0, 0)))
        + jnp.pad(from_prev, ((0, n_frames - BLK), (0, 0)))
    )
    grad_cat = jnp.concatenate(
        [query_grad.reshape(n_frames, QW), own_rows.astype(jnp.bfloat16)], axis=1
    )
    grad_scale = 1.0 / math.sqrt(dp_count * frames_total)
    per_seq = lax.psum_scatter(
        (
            lax.dot_general(
                modulated, grad_cat, (((0,), (0,)), ((), ())), preferred_element_type=jnp.float32
            )
            * grad_scale
        ).astype(jnp.bfloat16),
        "seq",
        scatter_dimension=0,
        tiled=True,
    ).astype(jnp.float32)
    weight_grad = lax.psum(per_seq, "dp")
    hidden_grad = lax.dot_general(
        grad_cat, weights_all, (((1,), (1,)), ((), ())), preferred_element_type=jnp.float32
    )
    scaled_grad = hidden_grad * gain_part
    frame_grad = (
        scaled_grad - normed * jnp.mean(scaled_grad * normed, axis=1, keepdims=True)
    ) / root_ms
    return (
        attn_blocks.reshape(n_frames, QW)[None],
        frame_grad.astype(jnp.bfloat16)[None],
        weight_grad[:, :QW],
        weight_grad[:, QW : 2 * QW],
        weight_grad[:, 2 * QW :],
    )


def solution(mesh):
    placed = (
        P("dp", "seq", None),
        P("dp", "seq", None),
        P("dp", "seq", None),
        P("dp"),
        P("dp"),
        P("seq", None),
        P(),
        P(),
        P("seq", None),
        P("seq", None),
        P("seq", None),
        P("dp", "seq", None),
    )
    return jax.shard_map(
        shards,
        mesh=mesh,
        in_specs=placed,
        out_specs=(
            P("dp", "seq", None),
            P("dp", "seq", None),
            P("seq", None),
            P("seq", None),
            P("seq", None),
        ),
        check_vma=False,
    )
```

profile of v0, /device:TPU:0, one launch (start us, length us, event | category | flops | bytes accessed | tf_op | source)
XLA Modules:
  0.0 271.2 jit_solution(1181808643607981817)
XLA Ops:
  7.2 0.7 all-gather.3.cloned.1.call-update
  8.0 1.6 pad_maximum_fusion.7
  11.0 0.8 copy.50
  12.8 0.9 dynamic-slice_add_fusion
  15.1 38.0 %all-gather.3.cloned.1.call-done = bf16[1664,512]{1,0:T(8,128)(2,1)} async-done(((bf16[104,512]{1,0:T(8,128)(2,1)}), bf16[1664,512]{1,0:T(8,128)(2,1)}) %all-gather.3.cloned.1.call-update) | async-done | bytes 1703952 | tf_op jit(solution)/shard_map/all_gather | solution.py:99
  53.0 2.4 gather_fusion
  55.5 0.9 gather_fusion.1
  56.9 43.3 %all-gather.5.cloned.1.call-done = bf16[1024,1536]{1,0:T(8,128)(2,1)} async-done(((bf16[64,1536]{1,0:T(8,128)(2,1)}), bf16[1024,1536]{1,0:T(8,128)(2,1)}) %all-gather.5.cloned.1.call-update) | async-done | bytes 3145744 | tf_op jit(solution)/shard_map/all_gather | solution.py:114
  100.2 2.6 convolution_convert_fusion
  102.9 1.3 collective-permute-start.1
  104.2 3.0 %collective-permute-start = (bf16[96,1024]{1,0:T(8,128)(2,1)S(1)}, bf16[96,1024]{1,0:T(8,128)(2,1)S(1)}, u32[]{:S(2)}, u32[]{:S(2)}) collective-permute-start(bf16[96,1024]{1,0:T(8,128)(2,1)S(1)} %slice.158), channel_id=1, source_target_pairs={{0,1},{1,2},{2,3},{3,4},{4,5},{5,6},{6,7},{7,8},{8,9},{9,10},{10,1... | collective-permute-start | bytes 589832 | tf_op jit(solution)/shard_map/ppermute | solution.py:17
  107.3 0.9 squeeze.30
  108.3 0.9 reshape.221
  109.3 0.7 reshape.220
  110.0 1.5 fusion.53
  111.5 1.3 copy.72
  112.8 2.1 copy.74
  114.8 1.0 copy.73
  115.8 1.0 copy.71
  116.7 1.0 copy.70
  118.0 1.0 copy.68
  119.3 3.3 %fusion.55 = (f32[3,8,48]{2,1,0:T(8,128)S(1)}, f32[3,8,48,192]{3,2,1,0:T(8,128)}) fusion(pred[3,48,192]{2,1,0:T(8,128)(4,1)S(1)} %or_and_fusion, bf16[3,48,8,64]{3,2,1,0:T(8,128)(2,1)} %reshape.221, bf16[3,48,8,64]{1,3,2,0:T(8,128)(2,1)S(1)} %bitcast.84, bf16[3,48,8,64]{1,3,2,0:T(8,128)(2,1)S(1)} %bitcast.81, bf16[3,48,8,64]{1,3,2,0:T(8,128)(2,1)} %bitcast.82, ...), kind=kOutput, calls=%fused_computation.98 | convolution fusion | flops 31776960 | bytes 1654272 | tf_op jit(solution)/shard_map/sub | solution.py:43
  122.6 2.1 convolution_bitcast_fusion
  124.8 2.0 fusion.24
  126.7 10.4 %convolution_bitcast_fusion.1 = f32[3,192,8,64]{1,3,2,0:T(8,128)} fusion(f32[3,8,48,192]{3,2,1,0:T(8,128)} %fusion.24, bf16[3,48,8,64]{3,2,1,0:T(8,128)(2,1)} %reshape.221, f32[3,8,48,192]{3,2,1,0:T(8,128)} %get-tuple-element.27, f32[3,8,48]{2,1,0:T(8,128)S(1)} %get-tuple-element.26), kind=kOutput, calls=%fused_computation.10 | convolution fusion | flops 29861184 | bytes 3101184 | tf_op jit(solution)/shard_map/bhqk,bqhd->bkhd/dot_general | solution.py:57
  137.2 3.5 %pad_maximum_fusion = f32[3,192,16,64]{1,3,2,0:T(8,128)} fusion(f32[3,192,8,64]{1,3,2,0:T(8,128)S(1)} %convolution_bitcast_fusion, f32[3,192,8,64]{1,3,2,0:T(8,128)} %convolution_bitcast_fusion.1), kind=kLoop, calls=%fused_computation.5 | loop fusion | flops 589824 | bytes 4718592 | tf_op jit(solution)/shard_map/concatenate | solution.py:63
  140.6 5.9 %copy.64 = f32[3,192,16,64]{3,2,1,0:T(8,128)} copy(f32[3,192,16,64]{1,3,2,0:T(8,128)} %pad_maximum_fusion) | data formatting | bytes 4718592 | tf_op jit(solution)/shard_map/concatenate | solution.py:63
  146.5 2.7 %slice_bitcast_fusion.3 = (f32[3,48,16,64]{3,2,1,0:T(8,128)S(1)}, f32[3,48,16,64]{3,2,1,0:T(8,128)S(1)}, f32[3,48,16,64]{3,2,1,0:T(8,128)S(1)}, f32[3,48,16,64]{3,2,1,0:T(8,128)S(1)}) fusion(f32[3,4,48,16,64]{4,3,2,1,0:T(8,128)} %bitcast.69), kind=kLoop, calls=%fused_computation.26 | loop fusion | bytes 4718592 | tf_op jit(solution)/shard_map/squeeze | solution.py:67
  149.6 0.7 copy-done.1
  150.7 1.4 copy-done.5
  152.1 1.0 slice.175
  153.1 2.2 slice.148
  155.3 1.6 collective-permute-start.2
  156.9 0.8 pad_add_fusion.1
  157.7 1.8 slice.150
  159.5 5.2 %collective-permute-start.3 = (f32[48,1024]{1,0:T(8,128)}, f32[48,1024]{1,0:T(8,128)}, u32[]{:S(2)}, u32[]{:S(2)}) collective-permute-start(f32[48,1024]{1,0:T(8,128)} %slice.150), channel_id=1, source_target_pairs={{0,1},{1,2},{2,3},{3,4},{4,5},{5,6},{6,7},{7,8},{8,9},{9,10},{10,1... | collective-permute-start | bytes 589832 | tf_op jit(solution)/shard_map/ppermute | solution.py:17
  164.8 10.3 %fusion.11 = bf16[3,48,8,64]{3,1,2,0:T(8,128)(2,1)S(1)} fusion(f32[3,8,48,192]{3,2,1,0:T(8,128)} %fusion.24, bf16[3,48,8,64]{1,3,2,0:T(8,128)(2,1)} %bitcast.85, bf16[3,48,8,64]{1,3,2,0:T(8,128)(2,1)} %bitcast.80, bf16[3,48,8,64]{1,3,2,0:T(8,128)(2,1)} %bitcast.83, bf16[3,48,8,64]{1,3,2,0:T(8,128)(2,1)} %bitcast.79, ...), kind=kOutput, calls=%fused_computation.28 | convolution fusion | flops 32294208 | bytes 2511360 | tf_op jit(solution)/shard_map/bhqk,bkhd->bqhd/dot_general | solution.py:54
  175.8 1.2 add_convert_fusion
  176.9 0.7 copy-done.23
  177.7 2.7 %multiply_convert_fusion = bf16[1024,1536]{1,0:T(8,128)(2,1)} fusion(bf16[144,1024]{1,0:T(8,128)(2,1)S(1)} %add_convert_fusion, bf16[144,512]{1,0:T(8,128)(2,1)S(1)} %reshape.222, f32[1024]{0:T(1024)S(1)} %bitcast.90, f32[1024]{0:T(1024)S(1)} %bitcast.87, f32[144,1024]{1,0:T(8,128)S(1)} %copy-done.7, f32[144]{0:T(256)S(1)} %copy-done.31), kind=kOutput, calls=%fused_computation.4 | convolution fusion | flops 457605120 | bytes 4186688 | tf_op jit(solution)/shard_map/dot_general | solution.py:159
  180.5 0.9 copy-done.11
  181.8 2.2 fusion.10
  184.0 0.9 broadcast_in_dim_reshape.4
  184.9 3.3 %multiply_reduce_fusion.1 = (f32[144]{0:T(256)S(1)}, f32[144,1024]{1,0:T(8,128)S(1)}) fusion(f32[144,1024]{1,0:T(8,128)S(1)} %copy-done.7, f32[144]{0:T(256)S(1)} %copy-done.32, f32[1024]{0:T(1024)S(1)} %bitcast.88, bf16[1024,1536]{1,0:T(8,128)(2,1)} %all-gather.5.cloned.1.call-done, bf16[144,1024]{1,0:T(8,128)(2,1)} %copy-done.23, ...), kind=kOutput, calls=%fused_computation.35 | convolution fusion | flops 454459264 | bytes 4772992 | tf_op jit(solution)/shard_map/dot_general | solution.py:169
  188.2 0.9 fusion.21
  189.1 59.4 %reduce-scatter.2.cloned.1.call-done = bf16[64,1536]{1,0:T(8,128)(2,1)} async-done(((bf16[1024,1536]{1,0:T(8,128)(2,1)}), bf16[64,1536]{1,0:T(8,128)(2,1)}) %reduce-scatter.2.cloned.1.call-update) | async-done | bytes 196624 | tf_op jit(solution)/shard_map/reduce_scatter | solution.py:157
  248.5 15.4 %all-reduce.7 = f32[64,1536]{1,0:T(8,128)S(1)} all-reduce(bf16[64,1536]{1,0:T(8,128)(2,1)} %reduce-scatter.2.cloned.1.call-done), channel_id=1, replica_groups=mesh['dp'=2,'seq'=16] {'dp'}, use_global_device_ids=true, to_apply=%region_8.9 | all-reduce | flops 98304 | bytes 589824 | tf_op jit(solution)/shard_map/psum | solution.py:168
  263.9 0.8 fusion.54
  (109 shorter events, 5.8 us)
Async XLA Ops:
  7.2 49.2 %copy-start = (bf16[512,1024]{1,0:T(8,128)(2,1)S(1)}, bf16[512,1024]{1,0:T(8,128)(2,1)}, u32[]{:S(2)}) copy-start(bf16[512,1024]{1,0:T(8,128)(2,1)} %param.18) | copy-start | bytes 3145732
  7.2 45.9 %all-gather.3.cloned.1.call-start = ((), (), s32[]{:S(2)}) async-start(), calls=%async_computation.1 | async-start | bytes 1810432 | tf_op jit(solution)/shard_map/all_gather | solution.py:99
  7.9 92.3 %all-gather.5.cloned.1.call-start = ((), (), s32[]{:S(2)}) async-start(), calls=%async_computation.2 | async-start | bytes 3342336 | tf_op jit(solution)/shard_map/all_gather | solution.py:114
  9.6 46.8 %copy-start.22 = (bf16[1,144,1024]{2,1,0:T(8,128)(2,1)S(1)}, bf16[1,144,1024]{2,1,0:T(8,128)(2,1)}, u32[]{:S(2)}) copy-start(bf16[1,144,1024]{2,1,0:T(8,128)(2,1)} %param.12) | copy-start | bytes 884740
  9.6 238.9 %reduce-scatter.2.cloned.1.call-start = ((), (), s32[]{:S(2)}) async-start(), calls=%async_computation.3 | async-start | bytes 3342336 | tf_op jit(solution)/shard_map/reduce_scatter | solution.py:157
  13.6 86.6 %copy-start.25 = (f32[1,1024]{1,0:T(1,128)}, f32[1,1024]{1,0:T(1,128)S(1)}, u32[]{:S(2)}) copy-start(f32[1,1024]{1,0:T(1,128)S(1)} %get-tuple-element.17) | copy-start | bytes 12292
  13.6 86.6 %copy-start.28 = (f32[1,1024]{1,0:T(1,128)}, f32[1,1024]{1,0:T(1,128)S(1)}, u32[]{:S(2)}) copy-start(f32[1,1024]{1,0:T(1,128)S(1)} %get-tuple-element.18) | copy-start | bytes 12292
  56.9 45.9 %copy-start.6 = (f32[144,1024]{1,0:T(8,128)}, f32[144,1024]{1,0:T(8,128)S(1)}, u32[]{:S(2)}) copy-start(f32[144,1024]{1,0:T(8,128)S(1)} %get-tuple-element.25) | copy-start | bytes 1769476
  56.9 43.3 %copy-start.30 = (f32[144]{0:T(256)}, f32[144]{0:T(256)S(1)}, u32[]{:S(2)}) copy-start(f32[144]{0:T(256)S(1)} %add_sqrt_fusion) | copy-start | bytes 1732
  100.2 7.1 %copy-start.24 = (bf16[1,144,512]{2,1,0:T(8,128)(2,1)S(1)}, bf16[1,144,512]{2,1,0:T(8,128)(2,1)}, u32[]{:S(2)}) copy-start(bf16[1,144,512]{2,1,0:T(8,128)(2,1)} %param.23) | copy-start | bytes 442372
  102.9 6.3 %collective-permute-start.1 = (bf16[48,1024]{1,0:T(8,128)(2,1)S(1)}, bf16[48,1024]{1,0:T(8,128)(2,1)S(1)}, u32[]{:S(2)}, u32[]{:S(2)}) collective-permute-start(bf16[48,1024]{1,0:T(8,128)(2,1)S(1)} %slice.160), channel_id=1, source_target_pairs={{1,0},{2,1},{3,2},{4,3},{5,4},{6,5},{7,6},{8,7},{9,8},{10,9},{11,1... | collective-permute-start | bytes 294920 | tf_op jit(solution)/shard_map/ppermute | solution.py:17
  104.2 5.0 %collective-permute-start = (bf16[96,1024]{1,0:T(8,128)(2,1)S(1)}, bf16[96,1024]{1,0:T(8,128)(2,1)S(1)}, u32[]{:S(2)}, u32[]{:S(2)}) collective-permute-start(bf16[96,1024]{1,0:T(8,128)(2,1)S(1)} %slice.158), channel_id=1, source_target_pairs={{0,1},{1,2},{2,3},{3,4},{4,5},{5,6},{6,7},{7,8},{8,9},{9,10},{10,1... | collective-permute-start | bytes 589832 | tf_op jit(solution)/shard_map/ppermute | solution.py:17
  111.5 3.3 %copy-start.9 = (bf16[3,48,1,8,64]{4,3,2,1,0:T(8,128)(2,1)S(1)}, bf16[3,48,1,8,64]{4,3,2,1,0:T(8,128)(2,1)}, u32[]{:S(2)}) copy-start(bf16[3,48,1,8,64]{4,3,2,1,0:T(8,128)(2,1)} %get-tuple-element.11) | copy-start | bytes 442372
  111.5 4.3 %copy-start.8 = (bf16[3,48,1,8,64]{4,3,2,1,0:T(8,128)(2,1)S(1)}, bf16[3,48,1,8,64]{4,3,2,1,0:T(8,128)(2,1)}, u32[]{:S(2)}) copy-start(bf16[3,48,1,8,64]{4,3,2,1,0:T(8,128)(2,1)} %get-tuple-element.12) | copy-start | bytes 442372
  112.7 6.6 %copy-start.18 = (bf16[3,48,1,8,64]{1,4,3,0,2:T(8,128)(2,1)}, bf16[3,48,1,8,64]{1,4,3,0,2:T(8,128)(2,1)S(1)}, u32[]{:S(2)}) copy-start(bf16[3,48,1,8,64]{1,4,3,0,2:T(8,128)(2,1)S(1)} %copy.72) | copy-start | bytes 442372
  117.7 1.6 copy-start.19
  118.0 6.7 %copy-start.14 = (bf16[3,48,1,8,64]{1,4,3,0,2:T(8,128)(2,1)}, bf16[3,48,1,8,64]{1,4,3,0,2:T(8,128)(2,1)S(1)}, u32[]{:S(2)}) copy-start(bf16[3,48,1,8,64]{1,4,3,0,2:T(8,128)(2,1)S(1)} %copy.69) | copy-start | bytes 442372
  119.3 3.3 %copy-start.20 = (bf16[3,48,1,8,64]{1,4,3,0,2:T(8,128)(2,1)}, bf16[3,48,1,8,64]{1,4,3,0,2:T(8,128)(2,1)S(1)}, u32[]{:S(2)}) copy-start(bf16[3,48,1,8,64]{1,4,3,0,2:T(8,128)(2,1)S(1)} %copy.75) | copy-start | bytes 442372
  122.6 4.1 %copy-start.33 = (f32[3,8,48]{2,1,0:T(8,128)}, f32[3,8,48]{2,1,0:T(8,128)S(1)}, u32[]{:S(2)}) copy-start(f32[3,8,48]{2,1,0:T(8,128)S(1)} %get-tuple-element.26) | copy-start | bytes 13828
  122.6 2.1 copy-start.10
  122.6 2.1 copy-start.12
  122.6 2.1 copy-start.16
  122.6 2.1 copy-start.21
  149.2 1.0 copy-start.1
  149.3 1.4 copy-start.3
  150.7 1.4 copy-start.5
  155.3 1.6 copy-start.2
  155.3 1.6 copy-start.4
  155.3 20.5 %collective-permute-start.2 = (f32[96,1024]{1,0:T(8,128)}, f32[96,1024]{1,0:T(8,128)}, u32[]{:S(2)}, u32[]{:S(2)}) collective-permute-start(f32[96,1024]{1,0:T(8,128)} %slice.148), channel_id=1, source_target_pairs={{1,0},{2,1},{3,2},{4,3},{5,4},{6,5},{7,6},{8,7},{9,8},{10,9},{11,1... | collective-permute-start | bytes 1179656 | tf_op jit(solution)/shard_map/ppermute | solution.py:17
  156.9 7.9 %copy-start.34 = (f32[3,8,48]{2,1,0:T(8,128)S(1)}, f32[3,8,48]{2,1,0:T(8,128)}, u32[]{:S(2)}) copy-start(f32[3,8,48]{2,1,0:T(8,128)} %copy-done.33) | copy-start | bytes 13828
  159.5 16.2 %collective-permute-start.3 = (f32[48,1024]{1,0:T(8,128)}, f32[48,1024]{1,0:T(8,128)}, u32[]{:S(2)}, u32[]{:S(2)}) collective-permute-start(f32[48,1024]{1,0:T(8,128)} %slice.150), channel_id=1, source_target_pairs={{0,1},{1,2},{2,3},{3,4},{4,5},{5,6},{6,7},{7,8},{8,9},{9,10},{10,1... | collective-permute-start | bytes 589832 | tf_op jit(solution)/shard_map/ppermute | solution.py:17
  164.8 10.6 %slice-start = ((f32[6,48,16,64]{3,2,1,0:T(8,128)}), f32[3,48,16,64]{3,2,1,0:T(8,128)S(1)}, s32[]{:S(2)}) async-start(f32[6,48,16,64]{3,2,1,0:T(8,128)} %copy-done.5), calls=%async_computation.4 | async-start | bytes 2359296 | tf_op jit(solution)/shard_map/slice | solution.py:147
  175.4 2.3 copy-start.7
  175.7 1.9 copy-start.26
  175.7 1.9 copy-start.29
  175.7 1.9 copy-start.31
  176.9 0.7 copy-start.23
  180.4 1.0 copy-start.11
  180.4 1.1 copy-start.13
  180.4 1.2 copy-start.15
  180.4 1.3 copy-start.17
  180.4 1.3 copy-start.35
  181.8 3.2 %copy-start.27 = (f32[1,1024]{1,0:T(1,128)S(1)}, f32[1,1024]{1,0:T(1,128)}, u32[]{:S(2)}) copy-start(f32[1,1024]{1,0:T(1,128)} %copy-done.25) | copy-start | bytes 12292
  181.8 3.2 %copy-start.32 = (f32[144]{0:T(256)S(1)}, f32[144]{0:T(256)}, u32[]{:S(2)}) copy-start(f32[144]{0:T(256)} %copy-done.30) | copy-start | bytes 1732
Sparse Core Ops, SparseCore 0:
  10.3 42.7 all-gather.2
  55.9 44.2 all-gather.4
  180.6 67.9 reduce-scatter.1
where the time goes:
time: 272 us; the launch traced here: 271 us
  waiting for transfers between devices  141 us (52%)
  matrix products  39.3 us (14%)
  local copies, waits for them, and re-layouts  36.5 us (13%)
  between operations  15.6 us (6%)
  blocking collectives  15.4 us (6%)
  other arithmetic  11.7 us (4%)
  starting transfers between devices  11.3 us (4%)
    reduce_scatter x1, waiting for transfers between devices, shards(): lax.psum_scatter((lax.dot_general(modulated, grad_cat, (((0,), (0,)), (()...  59.4 us
    all_gather x1, waiting for transfers between devices, shards(): weights_all = lax.all_gather(shard_cat, 'seq', axis=0, tiled=True)  43.3 us
    all_gather x1, waiting for transfers between devices, shards(): lax.all_gather(token_table, 'seq', axis=0, tiled=True)  38 us
    psum x1, blocking collectives, shards(): weight_grad = lax.psum(per_seq, 'dp')  15.4 us
    unnamed x80, local copies, waits for them, and re-layouts  12.5 us
    ppermute x4, starting transfers between devices, shifted(): return lax.ppermute(block, axis, route)  11.2 us
    dot_general x1, matrix products, attend_window(): jnp.einsum('bhqk,bqhd->bkhd', grad_scores, q_blocks, preferred_element_ty...  10.4 us
    dot_general x1, matrix products, attend_window(): jnp.einsum('bhqk,bkhd->bqhd', grad_scores, key_win, preferred_element_typ...  10.3 us
  transfers between devices with their start and end apart: 7, of which 3 were waited for; matrix products, arithmetic and copies ran while one was open for 12% of the time, Pallas kernels for 0%

commit v1 on v0

--- a/solution.py
+++ b/solution.py
@@ -165,7 +165,8 @@
         scatter_dimension=0,
         tiled=True,
     ).astype(jnp.float32)
-    weight_grad = lax.psum(per_seq, "dp")
+    v_now = jax.lax.ppermute(per_seq, "dp", [(0, 1), (1, 0)])
+    weight_grad = per_seq + v_now
     hidden_grad = lax.dot_general(
         grad_cat, weights_all, (((1,), (1,)), ((), ())), preferred_element_type=jnp.float32
     )

time: 272 us -> 267 us (0.982)
  blocking collectives: 15.4 us -> 0 us
  waiting for transfers between devices: 141 us -> 149 us
    psum x1 -> x0, blocking collectives: 15.4 us -> none  [shards(): weight_grad = lax.psum(per_seq, 'dp')]
    ppermute x0 -> x1, waiting for transfers between devices: none -> 6.58 us  [shards(): v_now = jax.lax.ppermute(per_seq, 'dp', [(0, 1), (1, 0)])]
    unnamed x80 -> x82, local copies, waits for them, and re-layouts: 12.5 us -> 12.5 us
  transfers between devices with their start and end apart: 7 -> 8, of which waited for: 3 -> 4; matrix products, arithmetic and copies ran while one was open for 12% -> 12% of each run, Pallas kernels for 0% -> 0%
where the time goes in v1:
time: 267 us; the launch traced here: 266 us
  waiting for transfers between devices  149 us (56%)
  matrix products  39.3 us (15%)
  local copies, waits for them, and re-layouts  36.5 us (14%)
  between operations  15.6 us (6%)
  starting transfers between devices  12.9 us (5%)
  other arithmetic  12.8 us (5%)
    reduce_scatter x1, waiting for transfers between devices, shards(): lax.psum_scatter((lax.dot_general(modulated, grad_cat, (((0,), (0,)), (()...  60.3 us
    all_gather x1, waiting for transfers between devices, shards(): weights_all = lax.all_gather(shard_cat, 'seq', axis=0, tiled=True)  43.3 us
    all_gather x1, waiting for transfers between devices, shards(): lax.all_gather(token_table, 'seq', axis=0, tiled=True)  38 us
    unnamed x82, local copies, waits for them, and re-layouts  12.5 us
    ppermute x4, starting transfers between devices, shifted(): return lax.ppermute(block, axis, route)  11.2 us
    dot_general x1, matrix products, attend_window(): jnp.einsum('bhqk,bqhd->bkhd', grad_scores, q_blocks, preferred_element_ty...  10.4 us
    dot_general x1, matrix products, attend_window(): jnp.einsum('bhqk,bkhd->bqhd', grad_scores, key_win, preferred_element_typ...  10.3 us
    ppermute x1, waiting for transfers between devices, shards(): v_now = jax.lax.ppermute(per_seq, 'dp', [(0, 1), (1, 0)])  6.58 us
  transfers between devices with their start and end apart: 8, of which 4 were waited for; matrix products, arithmetic and copies ran while one was open for 12% of the time, Pallas kernels for 0%

profile of v1, /device:TPU:0, one launch (start us, length us, event | category | flops | bytes accessed | tf_op | source)
XLA Modules:
  0.0 265.9 jit_solution(11017096866380035656)
XLA Ops:
  8.0 1.6 pad_maximum_fusion.7
  11.0 0.8 copy.50
  12.8 0.9 dynamic-slice_add_fusion
  15.1 38.0 %all-gather.3.cloned.1.call-done = bf16[1664,512]{1,0:T(8,128)(2,1)} async-done(((bf16[104,512]{1,0:T(8,128)(2,1)}), bf16[1664,512]{1,0:T(8,128)(2,1)}) %all-gather.3.cloned.1.call-update) | async-done | bytes 1703952 | tf_op jit(solution)/shard_map/all_gather | solution.py:99
  53.0 2.4 gather_fusion
  55.5 0.9 gather_fusion.1
  56.9 43.3 %all-gather.5.cloned.1.call-done = bf16[1024,1536]{1,0:T(8,128)(2,1)} async-done(((bf16[64,1536]{1,0:T(8,128)(2,1)}), bf16[1024,1536]{1,0:T(8,128)(2,1)}) %all-gather.5.cloned.1.call-update) | async-done | bytes 3145744 | tf_op jit(solution)/shard_map/all_gather | solution.py:114
  100.2 2.6 convolution_convert_fusion
  102.9 1.3 collective-permute-start.1
  104.2 3.0 %collective-permute-start = (bf16[96,1024]{1,0:T(8,128)(2,1)S(1)}, bf16[96,1024]{1,0:T(8,128)(2,1)S(1)}, u32[]{:S(2)}, u32[]{:S(2)}) collective-permute-start(bf16[96,1024]{1,0:T(8,128)(2,1)S(1)} %slice.158), channel_id=1, source_target_pairs={{0,1},{1,2},{2,3},{3,4},{4,5},{5,6},{6,7},{7,8},{8,9},{9,10},{10,1... | collective-permute-start | bytes 589832 | tf_op jit(solution)/shard_map/ppermute | solution.py:17
  107.3 0.9 squeeze.30
  108.3 0.9 reshape.221
  109.3 0.7 reshape.220
  110.0 1.4 fusion.53
  111.4 1.3 copy.72
  112.7 2.1 copy.74
  114.8 1.0 copy.73
  115.8 1.0 copy.71
  116.8 1.0 copy.70
  118.0 1.0 copy.68
  119.3 3.3 %fusion.55 = (f32[3,8,48]{2,1,0:T(8,128)S(1)}, f32[3,8,48,192]{3,2,1,0:T(8,128)}) fusion(pred[3,48,192]{2,1,0:T(8,128)(4,1)S(1)} %or_and_fusion, bf16[3,48,8,64]{3,2,1,0:T(8,128)(2,1)} %reshape.221, bf16[3,48,8,64]{1,3,2,0:T(8,128)(2,1)S(1)} %bitcast.84, bf16[3,48,8,64]{1,3,2,0:T(8,128)(2,1)S(1)} %bitcast.81, bf16[3,48,8,64]{1,3,2,0:T(8,128)(2,1)} %bitcast.82, ...), kind=kOutput, calls=%fused_computation.99 | convolution fusion | flops 31776960 | bytes 1654272 | tf_op jit(solution)/shard_map/sub | solution.py:43
  122.6 2.1 convolution_bitcast_fusion
  124.8 1.9 fusion.24
  126.7 10.4 %convolution_bitcast_fusion.1 = f32[3,192,8,64]{1,3,2,0:T(8,128)} fusion(f32[3,8,48,192]{3,2,1,0:T(8,128)} %fusion.24, bf16[3,48,8,64]{3,2,1,0:T(8,128)(2,1)} %reshape.221, f32[3,8,48,192]{3,2,1,0:T(8,128)} %get-tuple-element.27, f32[3,8,48]{2,1,0:T(8,128)S(1)} %get-tuple-element.26), kind=kOutput, calls=%fused_computation.10 | convolution fusion | flops 29861184 | bytes 3101184 | tf_op jit(solution)/shard_map/bhqk,bqhd->bkhd/dot_general | solution.py:57
  137.1 3.5 %pad_maximum_fusion = f32[3,192,16,64]{1,3,2,0:T(8,128)} fusion(f32[3,192,8,64]{1,3,2,0:T(8,128)S(1)} %convolution_bitcast_fusion, f32[3,192,8,64]{1,3,2,0:T(8,128)} %convolution_bitcast_fusion.1), kind=kLoop, calls=%fused_computation.5 | loop fusion | flops 589824 | bytes 4718592 | tf_op jit(solution)/shard_map/concatenate | solution.py:63
  140.6 5.9 %copy.64 = f32[3,192,16,64]{3,2,1,0:T(8,128)} copy(f32[3,192,16,64]{1,3,2,0:T(8,128)} %pad_maximum_fusion) | data formatting | bytes 4718592 | tf_op jit(solution)/shard_map/concatenate | solution.py:63
  146.5 2.7 %slice_bitcast_fusion.3 = (f32[3,48,16,64]{3,2,1,0:T(8,128)S(1)}, f32[3,48,16,64]{3,2,1,0:T(8,128)S(1)}, f32[3,48,16,64]{3,2,1,0:T(8,128)S(1)}, f32[3,48,16,64]{3,2,1,0:T(8,128)S(1)}) fusion(f32[3,4,48,16,64]{4,3,2,1,0:T(8,128)} %bitcast.69), kind=kLoop, calls=%fused_computation.26 | loop fusion | bytes 4718592 | tf_op jit(solution)/shard_map/squeeze | solution.py:67
  150.7 1.4 copy-done.5
  152.1 1.0 slice.175
  153.1 2.2 slice.148
  155.2 1.6 collective-permute-start.2
  156.9 0.8 pad_add_fusion.1
  157.7 1.8 slice.150
  159.5 5.3 %collective-permute-start.3 = (f32[48,1024]{1,0:T(8,128)}, f32[48,1024]{1,0:T(8,128)}, u32[]{:S(2)}, u32[]{:S(2)}) collective-permute-start(f32[48,1024]{1,0:T(8,128)} %slice.150), channel_id=1, source_target_pairs={{0,1},{1,2},{2,3},{3,4},{4,5},{5,6},{6,7},{7,8},{8,9},{9,10},{10,1... | collective-permute-start | bytes 589832 | tf_op jit(solution)/shard_map/ppermute | solution.py:17
  164.7 10.3 %fusion.11 = bf16[3,48,8,64]{3,1,2,0:T(8,128)(2,1)S(1)} fusion(f32[3,8,48,192]{3,2,1,0:T(8,128)} %fusion.24, bf16[3,48,8,64]{1,3,2,0:T(8,128)(2,1)} %bitcast.85, bf16[3,48,8,64]{1,3,2,0:T(8,128)(2,1)} %bitcast.80, bf16[3,48,8,64]{1,3,2,0:T(8,128)(2,1)} %bitcast.83, bf16[3,48,8,64]{1,3,2,0:T(8,128)(2,1)} %bitcast.79, ...), kind=kOutput, calls=%fused_computation.28 | convolution fusion | flops 32294208 | bytes 2511360 | tf_op jit(solution)/shard_map/bhqk,bkhd->bqhd/dot_general | solution.py:54
  175.8 1.2 add_convert_fusion
  176.9 0.7 copy-done.24
  177.7 2.7 %multiply_convert_fusion = bf16[1024,1536]{1,0:T(8,128)(2,1)} fusion(bf16[144,1024]{1,0:T(8,128)(2,1)S(1)} %add_convert_fusion, bf16[144,512]{1,0:T(8,128)(2,1)S(1)} %reshape.222, f32[1024]{0:T(1024)S(1)} %bitcast.90, f32[1024]{0:T(1024)S(1)} %bitcast.87, f32[144,1024]{1,0:T(8,128)S(1)} %copy-done.7, f32[144]{0:T(256)S(1)} %copy-done.32), kind=kOutput, calls=%fused_computation.4 | convolution fusion | flops 457605120 | bytes 4186688 | tf_op jit(solution)/shard_map/dot_general | solution.py:159
  180.4 0.9 copy-done.12
  181.8 2.2 fusion.10
  184.0 0.9 broadcast_in_dim_reshape.4
  184.9 3.3 %multiply_reduce_fusion.1 = (f32[144]{0:T(256)S(1)}, f32[144,1024]{1,0:T(8,128)S(1)}) fusion(f32[144,1024]{1,0:T(8,128)S(1)} %copy-done.7, f32[144]{0:T(256)S(1)} %copy-done.33, f32[1024]{0:T(1024)S(1)} %bitcast.88, bf16[1024,1536]{1,0:T(8,128)(2,1)} %all-gather.5.cloned.1.call-done, bf16[144,1024]{1,0:T(8,128)(2,1)} %copy-done.24, ...), kind=kOutput, calls=%fused_computation.35 | convolution fusion | flops 454459264 | bytes 4772992 | tf_op jit(solution)/shard_map/dot_general | solution.py:170
  188.2 60.3 %reduce-scatter.2.cloned.1.call-done = bf16[64,1536]{1,0:T(8,128)(2,1)} async-done(((bf16[1024,1536]{1,0:T(8,128)(2,1)}), bf16[64,1536]{1,0:T(8,128)(2,1)}) %reduce-scatter.2.cloned.1.call-update) | async-done | bytes 196624 | tf_op jit(solution)/shard_map/reduce_scatter | solution.py:157
  248.5 1.0 convert_element_type.71
  249.6 1.5 collective-permute-start.4
  251.1 0.9 fusion.21
  252.0 6.6 %collective-permute-done.4 = f32[64,1536]{1,0:T(8,128)S(1)} collective-permute-done((f32[64,1536]{1,0:T(8,128)S(1)}, f32[64,1536]{1,0:T(8,128)S(1)}, u32[]{:S(2)}, u32[]{:S(2)}) %collective-permute-start.4) | collective-permute-done | bytes 393248 | tf_op jit(solution)/shard_map/ppermute | solution.py:168
  258.6 0.8 fusion.54
  (114 shorter events, 7.2 us)
Async XLA Ops:
  7.2 49.2 %copy-start = (bf16[512,1024]{1,0:T(8,128)(2,1)S(1)}, bf16[512,1024]{1,0:T(8,128)(2,1)}, u32[]{:S(2)}) copy-start(bf16[512,1024]{1,0:T(8,128)(2,1)} %param.18) | copy-start | bytes 3145732
  7.2 45.9 %all-gather.3.cloned.1.call-start = ((), (), s32[]{:S(2)}) async-start(), calls=%async_computation.1 | async-start | bytes 1810432 | tf_op jit(solution)/shard_map/all_gather | solution.py:99
  7.9 92.3 %all-gather.5.cloned.1.call-start = ((), (), s32[]{:S(2)}) async-start(), calls=%async_computation.2 | async-start | bytes 3342336 | tf_op jit(solution)/shard_map/all_gather | solution.py:114
  9.6 46.8 %copy-start.23 = (bf16[1,144,1024]{2,1,0:T(8,128)(2,1)S(1)}, bf16[1,144,1024]{2,1,0:T(8,128)(2,1)}, u32[]{:S(2)}) copy-start(bf16[1,144,1024]{2,1,0:T(8,128)(2,1)} %param.12) | copy-start | bytes 884740
  9.6 238.9 %reduce-scatter.2.cloned.1.call-start = ((), (), s32[]{:S(2)}) async-start(), calls=%async_computation.3 | async-start | bytes 3342336 | tf_op jit(solution)/shard_map/reduce_scatter | solution.py:157
  13.6 86.6 %copy-start.26 = (f32[1,1024]{1,0:T(1,128)}, f32[1,1024]{1,0:T(1,128)S(1)}, u32[]{:S(2)}) copy-start(f32[1,1024]{1,0:T(1,128)S(1)} %get-tuple-element.17) | copy-start | bytes 12292
  13.6 86.6 %copy-start.29 = (f32[1,1024]{1,0:T(1,128)}, f32[1,1024]{1,0:T(1,128)S(1)}, u32[]{:S(2)}) copy-start(f32[1,1024]{1,0:T(1,128)S(1)} %get-tuple-element.18) | copy-start | bytes 12292
  56.9 45.9 %copy-start.6 = (f32[144,1024]{1,0:T(8,128)}, f32[144,1024]{1,0:T(8,128)S(1)}, u32[]{:S(2)}) copy-start(f32[144,1024]{1,0:T(8,128)S(1)} %get-tuple-element.25) | copy-start | bytes 1769476
  56.9 43.3 %copy-start.31 = (f32[144]{0:T(256)}, f32[144]{0:T(256)S(1)}, u32[]{:S(2)}) copy-start(f32[144]{0:T(256)S(1)} %add_sqrt_fusion) | copy-start | bytes 1732
  100.2 7.1 %copy-start.25 = (bf16[1,144,512]{2,1,0:T(8,128)(2,1)S(1)}, bf16[1,144,512]{2,1,0:T(8,128)(2,1)}, u32[]{:S(2)}) copy-start(bf16[1,144,512]{2,1,0:T(8,128)(2,1)} %param.23) | copy-start | bytes 442372
  102.9 6.3 %collective-permute-start.1 = (bf16[48,1024]{1,0:T(8,128)(2,1)S(1)}, bf16[48,1024]{1,0:T(8,128)(2,1)S(1)}, u32[]{:S(2)}, u32[]{:S(2)}) collective-permute-start(bf16[48,1024]{1,0:T(8,128)(2,1)S(1)} %slice.160), channel_id=1, source_target_pairs={{1,0},{2,1},{3,2},{4,3},{5,4},{6,5},{7,6},{8,7},{9,8},{10,9},{11,1... | collective-permute-start | bytes 294920 | tf_op jit(solution)/shard_map/ppermute | solution.py:17
  104.2 5.0 %collective-permute-start = (bf16[96,1024]{1,0:T(8,128)(2,1)S(1)}, bf16[96,1024]{1,0:T(8,128)(2,1)S(1)}, u32[]{:S(2)}, u32[]{:S(2)}) collective-permute-start(bf16[96,1024]{1,0:T(8,128)(2,1)S(1)} %slice.158), channel_id=1, source_target_pairs={{0,1},{1,2},{2,3},{3,4},{4,5},{5,6},{6,7},{7,8},{8,9},{9,10},{10,1... | collective-permute-start | bytes 589832 | tf_op jit(solution)/shard_map/ppermute | solution.py:17
  111.4 3.4 %copy-start.9 = (bf16[3,48,1,8,64]{4,3,2,1,0:T(8,128)(2,1)S(1)}, bf16[3,48,1,8,64]{4,3,2,1,0:T(8,128)(2,1)}, u32[]{:S(2)}) copy-start(bf16[3,48,1,8,64]{4,3,2,1,0:T(8,128)(2,1)} %get-tuple-element.11) | copy-start | bytes 442372
  111.4 4.4 %copy-start.8 = (bf16[3,48,1,8,64]{4,3,2,1,0:T(8,128)(2,1)S(1)}, bf16[3,48,1,8,64]{4,3,2,1,0:T(8,128)(2,1)}, u32[]{:S(2)}) copy-start(bf16[3,48,1,8,64]{4,3,2,1,0:T(8,128)(2,1)} %get-tuple-element.12) | copy-start | bytes 442372
  112.7 6.6 %copy-start.19 = (bf16[3,48,1,8,64]{1,4,3,0,2:T(8,128)(2,1)}, bf16[3,48,1,8,64]{1,4,3,0,2:T(8,128)(2,1)S(1)}, u32[]{:S(2)}) copy-start(bf16[3,48,1,8,64]{1,4,3,0,2:T(8,128)(2,1)S(1)} %copy.72) | copy-start | bytes 442372
  117.8 1.6 copy-start.20
  118.0 6.7 %copy-start.15 = (bf16[3,48,1,8,64]{1,4,3,0,2:T(8,128)(2,1)}, bf16[3,48,1,8,64]{1,4,3,0,2:T(8,128)(2,1)S(1)}, u32[]{:S(2)}) copy-start(bf16[3,48,1,8,64]{1,4,3,0,2:T(8,128)(2,1)S(1)} %copy.69) | copy-start | bytes 442372
  119.3 3.3 %copy-start.21 = (bf16[3,48,1,8,64]{1,4,3,0,2:T(8,128)(2,1)}, bf16[3,48,1,8,64]{1,4,3,0,2:T(8,128)(2,1)S(1)}, u32[]{:S(2)}) copy-start(bf16[3,48,1,8,64]{1,4,3,0,2:T(8,128)(2,1)S(1)} %copy.75) | copy-start | bytes 442372
  122.6 4.1 %copy-start.34 = (f32[3,8,48]{2,1,0:T(8,128)}, f32[3,8,48]{2,1,0:T(8,128)S(1)}, u32[]{:S(2)}) copy-start(f32[3,8,48]{2,1,0:T(8,128)S(1)} %get-tuple-element.26) | copy-start | bytes 13828
  122.6 2.1 copy-start.11
  122.6 2.1 copy-start.13
  122.6 2.1 copy-start.17
  122.6 2.1 copy-start.22
  149.2 1.0 copy-start.1
  149.2 1.4 copy-start.3
  150.7 1.4 copy-start.5
  155.2 1.6 copy-start.2
  155.2 1.6 copy-start.4
  155.2 20.5 %collective-permute-start.2 = (f32[96,1024]{1,0:T(8,128)}, f32[96,1024]{1,0:T(8,128)}, u32[]{:S(2)}, u32[]{:S(2)}) collective-permute-start(f32[96,1024]{1,0:T(8,128)} %slice.148), channel_id=1, source_target_pairs={{1,0},{2,1},{3,2},{4,3},{5,4},{6,5},{7,6},{8,7},{9,8},{10,9},{11,1... | collective-permute-start | bytes 1179656 | tf_op jit(solution)/shard_map/ppermute | solution.py:17
  156.9 7.9 %copy-start.35 = (f32[3,8,48]{2,1,0:T(8,128)S(1)}, f32[3,8,48]{2,1,0:T(8,128)}, u32[]{:S(2)}) copy-start(f32[3,8,48]{2,1,0:T(8,128)} %copy-done.34) | copy-start | bytes 13828
  159.5 16.3 %collective-permute-start.3 = (f32[48,1024]{1,0:T(8,128)}, f32[48,1024]{1,0:T(8,128)}, u32[]{:S(2)}, u32[]{:S(2)}) collective-permute-start(f32[48,1024]{1,0:T(8,128)} %slice.150), channel_id=1, source_target_pairs={{0,1},{1,2},{2,3},{3,4},{4,5},{5,6},{6,7},{7,8},{8,9},{9,10},{10,1... | collective-permute-start | bytes 589832 | tf_op jit(solution)/shard_map/ppermute | solution.py:17
  164.7 10.6 %slice-start = ((f32[6,48,16,64]{3,2,1,0:T(8,128)}), f32[3,48,16,64]{3,2,1,0:T(8,128)S(1)}, s32[]{:S(2)}) async-start(f32[6,48,16,64]{3,2,1,0:T(8,128)} %copy-done.5), calls=%async_computation.4 | async-start | bytes 2359296 | tf_op jit(solution)/shard_map/slice | solution.py:147
  175.3 2.3 copy-start.7
  175.7 1.9 copy-start.27
  175.7 1.9 copy-start.30
  175.7 1.9 copy-start.32
  176.9 0.7 copy-start.24
  180.4 1.0 copy-start.12
  180.4 1.1 copy-start.14
  180.4 1.2 copy-start.16
  180.4 1.3 copy-start.18
  180.4 1.3 copy-start.36
  181.8 3.2 %copy-start.28 = (f32[1,1024]{1,0:T(1,128)S(1)}, f32[1,1024]{1,0:T(1,128)}, u32[]{:S(2)}) copy-start(f32[1,1024]{1,0:T(1,128)} %copy-done.26) | copy-start | bytes 12292
  181.8 3.2 %copy-start.33 = (f32[144]{0:T(256)S(1)}, f32[144]{0:T(256)}, u32[]{:S(2)}) copy-start(f32[144]{0:T(256)} %copy-done.31) | copy-start | bytes 1732
  248.5 10.0 %copy-start.10 = (bf16[64,1536]{1,0:T(8,128)(2,1)S(1)}, bf16[64,1536]{1,0:T(8,128)(2,1)}, u32[]{:S(2)}) copy-start(bf16[64,1536]{1,0:T(8,128)(2,1)} %reduce-scatter.2.cloned.1.call-done) | copy-start | bytes 589828
  249.6 9.0 %collective-permute-start.4 = (f32[64,1536]{1,0:T(8,128)S(1)}, f32[64,1536]{1,0:T(8,128)S(1)}, u32[]{:S(2)}, u32[]{:S(2)}) collective-permute-start(f32[64,1536]{1,0:T(8,128)S(1)} %convert_element_type.71), channel_id=1, source_target_pairs={{0,16},{16,0},{1,17},{17,1},{2,18},{18,2},{3,19},{19,3},{4,20},{20... | collective-permute-start | bytes 1179656 | tf_op jit(solution)/shard_map/ppermute | solution.py:168
Sparse Core Ops, SparseCore 0:
  10.3 42.7 all-gather.2
  55.9 44.2 all-gather.4
  180.6 67.9 reduce-scatter.1
